TPU v7x, 128 devices: a whole 4x4x4 slice. The times are simulated.
128 devices in a mesh: owner: 16 (over y, z), kvh: 8 (over x, core).
Axes of the slice: x: 4, y: 4, z: 4, core: 2. Of those that a mesh axis runs over, the one named last changes fastest.
Arguments:
- queries: bfloat16 [32, 32, 64, 128], P('owner', None, 'kvh'), may hold values from -6 to 6
- new_keys: bfloat16 [32, 32, 8, 128], P('owner', None, 'kvh'), may hold values from -6 to 6
- new_values: bfloat16 [32, 32, 8, 128], P('owner', None, 'kvh'), may hold values from -6 to 6
- ancestors: int32 [32, 32], P('owner'), may hold values from 0 to 95, as said below
- tile_keys: bfloat16 [96, 8, 512, 128], P('owner', 'kvh'), may hold values from -6 to 6
- tile_values: bfloat16 [96, 8, 512, 128], P('owner', 'kvh'), may hold values from -6 to 6
- tile_lengths: int32 [96], P('owner'), may hold values from 2 to 512
- out_weight: bfloat16 [8192, 8192], P('kvh'), may hold values from -0.0625 to 0.0625
Outputs:
- mixed: bfloat16 [1024, 8192], P(('owner', 'kvh'))
Inputs may be any that keep to these rules, and one draw needn't show every extreme that they name: `ancestors`: each row names 32 different tiles.
All inputs are finite; a program needn't handle non-finite values.
Results may differ from a plain program's by a relative error of at most 0.017.
Values may be sent and summed in bfloat16 or wider, within the bound.
No kernel may reach another device: no remote copies, remote signals or barrier semaphores. Data moves between devices by JAX's collectives and lax.ppermute only.
A program may use at most 320 MiB of HBM per device.

v0:
```python
import jax
import jax.numpy as jnp
from jax import lax
from jax.sharding import PartitionSpec as P

NEG = -1e30


def from_everyone(x, axis):
    copies = jnp.broadcast_to(x, (lax.axis_size(axis), *x.shape))
    return lax.all_to_all(copies, axis, split_axis=0, concat_axis=0, tiled=True)


def laid_out(parts, dim):
    shape = list(parts.shape[1:])
    shape[dim] *= parts.shape[0]
    return jnp.moveaxis(parts, 0, dim).reshape(shape)


def gathered_copies(x, axis, dim):
    parts = from_everyone(x, axis)
    return laid_out(parts, dim)


def in_one_piece(arrays, axis, dim, along):
    columns = [a.reshape(*a.shape[:along], -1) for a in arrays]
    both = jnp.concatenate(columns, axis=along)
    result, at, finished = (gathered_copies(both, axis, dim), 0, [])
    for a, column in zip(arrays, columns):
        section = result[..., at : at + column.shape[along]]
        finished.append(section.reshape(*section.shape[:along], *a.shape[along:]))
        at += column.shape[along]
    return tuple(finished)


def sent_together(arrays, axis, split_dim, concat_dim, along):
    ends, at = ([], 0)
    for a in arrays[:-1]:
        at += a.shape[along]
        ends.append(at)
    both = jnp.concatenate(arrays, axis=along)
    return tuple(
        jnp.split(
            lax.all_to_all(both, axis, split_axis=split_dim, concat_axis=concat_dim, tiled=True),
            ends,
            axis=along,
        )
    )


def cut_along(x, dim, count):
    shape = x.shape
    parts = x.reshape(*shape[:dim], count, shape[dim] // count, *shape[dim + 1 :])
    return jnp.moveaxis(parts, dim, 0)


def sent_and_summed(x, axis, dim):
    parts = cut_along(x, dim, lax.axis_size(axis))
    arrived = lax.all_to_all(parts, axis, split_axis=0, concat_axis=0, tiled=True)
    return arrived.astype(jnp.float32).sum(axis=0)


def owner_partial(qrows, keys, values, live, member):
    count_p, rows, width = qrows.shape
    count, size = (keys.shape[0], keys.shape[1])
    flat = qrows.reshape(count_p * rows, width)
    scores = jnp.dot(
        flat, keys.reshape(count * size, width).T, preferred_element_type=jnp.float32
    ) * width ** (-0.5)
    scores = scores.reshape(count_p, rows, count * size)
    valid = jnp.repeat(member, size, axis=1)[:, None, :] & live.reshape(count * size)[None, None, :]
    masked = jnp.where(valid, scores, NEG)
    peak = jnp.max(masked, axis=2)
    weights = jnp.where(valid, jnp.exp(masked - peak[..., None]), 0.0)
    total = jnp.sum(weights, axis=2)
    summed = jnp.dot(
        weights.astype(jnp.bfloat16).reshape(count_p * rows, count * size),
        values.reshape(count * size, width),
        preferred_element_type=jnp.float32,
    )
    summed = summed.reshape(count_p, rows, width)
    safe = jnp.where(total > 0, total, 1.0)
    average = jnp.where(total[..., None] > 0, summed / safe[..., None], 0.0).astype(jnp.bfloat16)
    return (average, peak, total)


def self_partial(query, keys, values):
    count_p, new, group, width = query.shape
    scores = jnp.einsum(
        "ntgh,nsh->ntgs", query, keys, preferred_element_type=jnp.float32
    ) * width ** (-0.5)
    steps = jnp.arange(new)
    causal = (steps[:, None] >= steps[None, :])[None, :, None, :]
    masked = jnp.where(causal, scores, NEG)
    peak = jnp.max(masked, axis=3)
    weights = jnp.where(causal, jnp.exp(masked - peak[..., None]), 0.0)
    total = jnp.sum(weights, axis=3)
    summed = jnp.einsum(
        "ntgs,nsh->ntgh", weights.astype(jnp.bfloat16), values, preferred_element_type=jnp.float32
    )
    rows = new * group
    return (
        summed.reshape(count_p, rows, width),
        peak.reshape(count_p, rows),
        total.reshape(count_p, rows),
    )


def combine(own, average, peak, total):
    own_sum, own_peak, own_total = own
    top = jnp.maximum(own_peak, jnp.max(peak, axis=0))
    own_factor = jnp.exp(own_peak - top)
    factor = total * jnp.exp(peak - top[None])
    denom = own_total * own_factor + jnp.sum(factor, axis=0)
    numer = own_sum * own_factor[..., None] + jnp.sum(
        factor[..., None] * average.astype(jnp.float32), axis=0
    )
    return (numer / denom[..., None]).astype(jnp.bfloat16)


def local(
    queries, new_keys, new_values, ancestors, tile_keys, tile_values, tile_lengths, out_weight
):
    owners = lax.axis_size("owner")
    part_dev, new, group, width = queries.shape
    per_owner, size = (tile_keys.shape[0], tile_keys.shape[2])
    tiles = per_owner * owners
    rows = new * group
    qrows = queries.reshape(part_dev, rows, width)
    own = self_partial(queries, new_keys[:, :, 0], new_values[:, :, 0])
    member = jnp.any(
        ancestors[:, :, None] == jnp.arange(tiles, dtype=jnp.int32)[None, None, :], axis=1
    )
    live = (jnp.arange(size, dtype=jnp.int32)[None, :] < tile_lengths[:, None]).astype(jnp.bfloat16)
    shared_q, shared_member = in_one_piece((qrows, member.astype(jnp.bfloat16)), "owner", 0, 1)
    mine = lax.axis_index("owner") * per_owner
    columns = lax.dynamic_slice_in_dim(shared_member, mine, per_owner, 1) > 0.5
    average, peak, total = owner_partial(
        shared_q, tile_keys[:, 0], tile_values[:, 0], live > 0.5, columns
    )
    average = lax.all_to_all(
        average.reshape(owners, part_dev, rows, width),
        "owner",
        split_axis=0,
        concat_axis=0,
        tiled=True,
    )
    peak, total = sent_together(
        (peak.reshape(owners, part_dev, rows), total.reshape(owners, part_dev, rows)),
        "owner",
        0,
        0,
        1,
    )
    attention = combine(own, average, peak, total)
    flat_attention = attention.reshape(part_dev * new, group * width)
    return sent_and_summed(
        jnp.dot(flat_attention, out_weight, preferred_element_type=jnp.float32).astype(
            jnp.bfloat16
        ),
        "kvh",
        0,
    ).astype(jnp.bfloat16)


def solution(mesh):
    return jax.shard_map(
        local,
        mesh=mesh,
        in_specs=(
            P("owner", None, "kvh", None),
            P("owner", None, "kvh", None),
            P("owner", None, "kvh", None),
            P("owner", None),
            P("owner", "kvh", None, None),
            P("owner", "kvh", None, None),
            P("owner"),
            P("kvh", None),
        ),
        out_specs=P(("owner", "kvh"), None),
        check_vma=False,
    )
```

profile of v0, /device:TPU:1, one launch (start us, length us, event | category | flops | bytes accessed | tf_op | source)
XLA Modules:
  0.0 231.2 jit_solution(14552935776647379768)
XLA Ops:
  0.0 1.1 copy.17
  1.1 0.8 fusion.16
  2.0 2.4 %broadcast_in_dim.80 = bf16[16,2,32864]{2,1,0:T(2,128)(2,1)} broadcast(bf16[2,32864]{1,0:T(2,128)(2,1)S(1)} %pad_maximum_fusion), dimensions={1,2} | broadcast | bytes 2234752 | tf_op jit(solution)/shard_map/broadcast_in_dim | solution.py:10
  4.5 8.6 %all-to-all-start = ((bf16[16,2,32864]{2,1,0:T(2,128)(2,1)}), bf16[16,2,32864]{2,1,0:T(2,128)(2,1)S(1)}, u32[]{:S(2)}, u32[]{:S(2)}) async-start(bf16[16,2,32864]{2,1,0:T(2,128)(2,1)} %broadcast_in_dim.80), calls=%async_computation | async-start | bytes 4210688 | tf_op jit(solution)/shard_map/all_to_all | solution.py:11
  13.1 0.7 fusion.20
  13.8 27.2 %all-to-all-done = bf16[16,2,32864]{2,1,0:T(2,128)(2,1)S(1)} async-done(((bf16[16,2,32864]{2,1,0:T(2,128)(2,1)}), bf16[16,2,32864]{2,1,0:T(2,128)(2,1)S(1)}, u32[]{:S(2)}, u32[]{:S(2)}) %all-to-all-start) | async-done | bytes 2103328 | tf_op jit(solution)/shard_map/all_to_all | solution.py:11
  41.1 2.7 %reshape.155 = bf16[32,32864]{1,0:T(8,128)(2,1)} reshape(bf16[16,2,32864]{2,1,0:T(2,128)(2,1)S(1)} %all-to-all-done) | data formatting | bytes 4206592 | tf_op jit(solution)/shard_map/reshape | solution.py:17
  44.5 3.0 %slice.9 = bf16[32,32768]{1,0:T(8,128)(2,1)} slice(bf16[32,32864]{1,0:T(8,128)(2,1)} %reshape.155), slice={[0:32], [0:32768]} | slice | bytes 4194304 | tf_op jit(solution)/shard_map/slice | solution.py:30
  47.7 2.9 %reshape_reshape.7 = bf16[8192,128]{1,0:T(8,128)(2,1)S(1)} reshape(bf16[32,32768]{1,0:T(8,128)(2,1)} %slice.9) | data formatting | bytes 4194304 | tf_op jit(solution)/shard_map/reshape;reshape | solution.py:66
  50.7 35.0 %fusion = (f32[8192]{0:T(1024)S(1)}, f32[8192,3072]{1,0:T(8,128)}) fusion(pred[32,3072]{1,0:T(8,128)(4,1)S(1)} %broadcast_and_fusion, bf16[8192,128]{1,0:T(8,128)(2,1)S(1)} %reshape_reshape.7, bf16[3072,128]{1,0:T(8,128)(2,1)S(1)} %bitcast.57), kind=kOutput, calls=%fused_computation.2 | convolution fusion | flops 6517940224 | bytes 103677952 | tf_op jit(solution)/shard_map/dot_general | solution.py:67
  85.7 49.4 %fusion.1 = (bf16[8192,3072]{1,0:T(8,128)(2,1)}, f32[8192]{0:T(1024)S(1)}) fusion(f32[8192,3072]{1,0:T(8,128)} %get-tuple-element.14, f32[8192]{0:T(1024)S(1)} %get-tuple-element.13, pred[32,3072]{1,0:T(8,128)(4,1)S(1)} %broadcast_and_fusion), kind=kLoop, calls=%fused_computation.3 | loop fusion | flops 150986752 | bytes 151158784 | tf_op jit(solution)/shard_map/convert_element_type | solution.py:77
  135.9 3.9 %all-to-all-start.1 = ((f32[16,4,256]{2,1,0:T(4,128)}), f32[16,4,256]{2,1,0:T(4,128)S(1)}, u32[]{:S(2)}, u32[]{:S(2)}) async-start(f32[16,4,256]{2,1,0:T(4,128)} %pad_maximum_fusion.1), calls=%async_computation.1 | async-start | bytes 131072 | tf_op jit(solution)/shard_map/all_to_all | solution.py:44
  139.8 22.0 %select_convert_fusion = bf16[32,256,128]{2,1,0:T(8,128)(2,1)} fusion(bf16[32,256,3072]{2,1,0:T(8,128)(2,1)} %bitcast.58, bf16[3072,128,1]{1,0,2:T(8,128)(2,1)S(1)} %bitcast.65, f32[32,256]{1,0:T(8,128)S(1)} %broadcast_select_fusion, pred[32,256]{1,0:T(8,128)(4,1)S(1)} %broadcast_compare_fusion), kind=kOutput, calls=%fused_computation.8 | convolution fusion | flops 6445596672 | bytes 53256192 | tf_op jit(solution)/shard_map/dot_general | solution.py:76
  161.8 6.7 %all-to-all-start.2 = ((bf16[16,2,256,128]{3,2,1,0:T(8,128)(2,1)}), bf16[16,2,256,128]{3,2,1,0:T(8,128)(2,1)S(1)}, u32[]{:S(2)}, u32[]{:S(2)}) async-start(bf16[16,2,256,128]{3,2,1,0:T(8,128)(2,1)} %bitcast.59), calls=%async_computation.2 | async-start | bytes 4194304 | tf_op jit(solution)/shard_map/all_to_all | solution.py:141
  169.6 0.9 div.21
  170.5 1.0 div.22
  171.5 0.8 mul.49
  172.3 1.7 mul.50
  174.0 19.5 %all-to-all-done.2 = bf16[16,2,256,128]{3,2,1,0:T(8,128)(2,1)S(1)} async-done(((bf16[16,2,256,128]{3,2,1,0:T(8,128)(2,1)}), bf16[16,2,256,128]{3,2,1,0:T(8,128)(2,1)S(1)}, u32[]{:S(2)}, u32[]{:S(2)}) %all-to-all-start.2) | async-done | bytes 2097184 | tf_op jit(solution)/shard_map/all_to_all | solution.py:141
  193.5 1.9 multiply_reduce_fusion
  195.4 1.0 reduce_sum.55
  196.4 8.9 %fusion.3 = bf16[8,8,8192]{2,1,0:T(8,128)(2,1)S(1)} fusion(bf16[1024,8192]{1,0:T(8,128)(2,1)} %param.15, f32[64,1024]{1,0:T(8,128)S(1)} %div.22, f32[64,1024]{1,0:T(8,128)S(1)} %reduce_sum.55, f32[64,1024]{1,0:T(8,128)} %mul.50, f32[8,8,8,128]{3,2,1,0:T(8,128)S(1)} %bitcast.60), kind=kOutput, calls=%fused_computation.6 | convolution fusion | flops 1074528256 | bytes 18874368 | tf_op jit(solution)/shard_map/dot_general | solution.py:158
  205.3 25.0 %all_to_all.20 = bf16[8,8,8192]{2,1,0:T(8,128)(2,1)S(1)} all-to-all(bf16[8,8,8192]{2,1,0:T(8,128)(2,1)S(1)} %fusion.3), channel_id=1, replica_groups=mesh['owner'=16,'kvh'=8] {'kvh'}, dimensions={0} | all-to-all | bytes 2097152 | tf_op jit(solution)/shard_map/all_to_all | solution.py:59
  230.3 0.8 reduce_sum.58
  (37 shorter events, 3.0 us)
Async XLA Ops:
  0.0 50.7 %copy-start = (bf16[6,1,512,128]{3,2,1,0:T(8,128)(2,1)S(1)}, bf16[6,1,512,128]{3,2,1,0:T(8,128)(2,1)}, u32[]{:S(2)}) copy-start(bf16[6,1,512,128]{3,2,1,0:T(8,128)(2,1)} %param.12) | copy-start | bytes 2359300
  4.5 36.6 %all-to-all-start = ((bf16[16,2,32864]{2,1,0:T(2,128)(2,1)}), bf16[16,2,32864]{2,1,0:T(2,128)(2,1)S(1)}, u32[]{:S(2)}, u32[]{:S(2)}) async-start(bf16[16,2,32864]{2,1,0:T(2,128)(2,1)} %broadcast_in_dim.80), calls=%async_computation | async-start | bytes 4210688 | tf_op jit(solution)/shard_map/all_to_all | solution.py:11
  85.7 54.0 %copy-start.5 = (bf16[6,1,512,128]{3,2,1,0:T(8,128)(2,1)S(1)}, bf16[6,1,512,128]{3,2,1,0:T(8,128)(2,1)}, u32[]{:S(2)}) copy-start(bf16[6,1,512,128]{3,2,1,0:T(8,128)(2,1)} %param.13) | copy-start | bytes 2359300
  135.9 25.9 %all-to-all-start.1 = ((f32[16,4,256]{2,1,0:T(4,128)}), f32[16,4,256]{2,1,0:T(4,128)S(1)}, u32[]{:S(2)}, u32[]{:S(2)}) async-start(f32[16,4,256]{2,1,0:T(4,128)} %pad_maximum_fusion.1), calls=%async_computation.1 | async-start | bytes 131072 | tf_op jit(solution)/shard_map/all_to_all | solution.py:44
  139.8 28.7 %copy-start.2 = (bf16[2,32,8,128]{3,2,1,0:T(8,128)(2,1)S(1)}, bf16[2,32,8,128]{3,2,1,0:T(8,128)(2,1)}, u32[]{:S(2)}) copy-start(bf16[2,32,8,128]{3,2,1,0:T(8,128)(2,1)} %param.8) | copy-start | bytes 393220
  139.8 28.7 %copy-start.3 = (bf16[2,32,1,128]{3,1,2,0:T(8,128)(2,1)S(1)}, bf16[2,32,1,128]{3,1,2,0:T(8,128)(2,1)}, u32[]{:S(2)}) copy-start(bf16[2,32,1,128]{3,1,2,0:T(8,128)(2,1)} %param.9) | copy-start | bytes 49156
  139.8 29.4 %copy-start.4 = (bf16[2,32,1,128]{3,1,2,0:T(8,128)(2,1)S(1)}, bf16[2,32,1,128]{3,1,2,0:T(8,128)(2,1)}, u32[]{:S(2)}) copy-start(bf16[2,32,1,128]{3,1,2,0:T(8,128)(2,1)} %param.10) | copy-start | bytes 49156
  161.8 31.7 %all-to-all-start.2 = ((bf16[16,2,256,128]{3,2,1,0:T(8,128)(2,1)}), bf16[16,2,256,128]{3,2,1,0:T(8,128)(2,1)S(1)}, u32[]{:S(2)}, u32[]{:S(2)}) async-start(bf16[16,2,256,128]{3,2,1,0:T(8,128)(2,1)} %bitcast.59), calls=%async_computation.2 | async-start | bytes 4194304 | tf_op jit(solution)/shard_map/all_to_all | solution.py:141
  168.5 62.7 %copy-start.1 = (bf16[6,1,512,128]{3,2,1,0:T(8,128)(2,1)S(1)}, bf16[6,1,512,128]{3,2,1,0:T(8,128)(2,1)}, u32[]{:S(2)}) copy-start(bf16[6,1,512,128]{3,2,1,0:T(8,128)(2,1)} %param.12) | copy-start | bytes 2359300
where the time goes:
time: 232 us; the launch traced here: 231 us
  matrix products  66.4 us (29%)
  other arithmetic  54.9 us (24%)
  waiting for transfers between devices  46.7 us (20%)
  blocking collectives  25 us (11%)
  starting transfers between devices  19.1 us (8%)
  local copies, waits for them, and re-layouts  18.7 us (8%)
    convert_element_type x1, other arithmetic, owner_partial(): weights.astype(jnp.bfloat16).reshape(count_p * rows, count * size)  49.4 us
    dot_general x1, matrix products, owner_partial(): jnp.dot(flat, keys.reshape(count * size, width).T, preferred_element_type...  35 us
    all_to_all x1, waiting for transfers between devices, from_everyone(): return lax.all_to_all(copies, axis, split_axis=0, concat_axis=0, tiled=True)  27.2 us
    all_to_all x1, blocking collectives, sent_and_summed(): lax.all_to_all(parts, axis, split_axis=0, concat_axis=0, tiled=True)  25 us
    dot_general x1, matrix products, owner_partial(): jnp.dot(weights.astype(jnp.bfloat16).reshape(count_p * rows, count * size...  22 us
    all_to_all x1, waiting for transfers between devices, local(): lax.all_to_all(average.reshape(owners, part_dev, rows, width), 'owner', s...  19.5 us
    dot_general x1, matrix products, local(): jnp.dot(flat_attention, out_weight, preferred_element_type=jnp.float32)  8.87 us
    all_to_all x1, starting transfers between devices, from_everyone(): return lax.all_to_all(copies, axis, split_axis=0, concat_axis=0, tiled=True)  8.6 us
  transfers between devices with their start and end apart: 3, of which 2 were waited for; matrix products, arithmetic and copies ran while one was open for 12% of the time, Pallas kernels for 0%

commit v1 on v0

v1 whole, which is shorter than its diff:
```python
import functools
import math

import jax
import jax.numpy as jnp
from jax import lax
from jax.experimental import pallas as pl
from jax.experimental.pallas import tpu as pltpu
from jax.sharding import PartitionSpec as P

NEG = -1e30
CHUNKS = 2
META = 16
STEP = 128
F32 = jnp.float32
BF16 = jnp.bfloat16


def to_lanes(column, count):
    r = lax.broadcasted_iota(jnp.int32, (128, 128), 0)
    c = lax.broadcasted_iota(jnp.int32, (128, 128), 1)
    eye = r == c
    rows = []
    for b in range(count // 128):
        wide = jnp.broadcast_to(column[b * 128 : (b + 1) * 128], (128, 128))
        rows.append(jnp.sum(jnp.where(eye, wide, 0.0), axis=0, keepdims=True))
    return rows


def attend_kernel(scale, halves, member, widths, q_ref, k_ref, v_ref, o_ref, m_ref, acc_ref):
    homes = q_ref.shape[0]
    rows = q_ref.shape[1] - META
    tiles, size = k_ref.shape[0], k_ref.shape[1]
    part = rows // halves
    which = lax.broadcasted_iota(jnp.int32, (rows, 1), 0) // part

    def one_tile(h, t, width):
        q = q_ref[h, :rows, :]
        s = lax.dot_general(q, k_ref[t, :width, :], (((1,), (1,)), ((), ())), preferred_element_type=F32)
        flag = jnp.zeros((rows, 1), F32)
        for i in range(halves):
            flag = jnp.where(which == i, member[(h * halves + i) * tiles + t].astype(F32), flag)
        inside = flag > 0.5
        old = m_ref[...]
        new = jnp.where(inside, jnp.maximum(old, jnp.max(s, axis=1, keepdims=True)), old)
        shift = jnp.where(inside, new * scale, -NEG)
        p = jnp.exp2(s * scale - shift).astype(BF16)
        alpha = jnp.exp2((old - new) * scale)
        m_ref[...] = new
        acc_ref[...] = acc_ref[...] * alpha + jnp.dot(p, v_ref[t, :width, :], preferred_element_type=F32)

    @pl.loop(0, homes)
    def _(h):
        m_ref[...] = jnp.full(m_ref.shape, NEG, F32)
        acc_ref[...] = jnp.zeros(acc_ref.shape, F32)

        @pl.loop(0, tiles)
        def _(t):
            used = member[h * halves * tiles + t]
            for i in range(1, halves):
                used = used + member[(h * halves + i) * tiles + t]
            steps = jnp.where(used > 0, widths[t], 0)
            for n in range(1, size // STEP + 1):

                @pl.when(steps == n)
                def _():
                    one_tile(h, t, n * STEP)

        total = acc_ref[:, 128:129]
        some = total > 0.0
        safe = jnp.where(some, total, 1.0)
        o_ref[h, :rows, :] = jnp.where(some, acc_ref[:, :128] / safe, 0.0).astype(BF16)
        level = jnp.where(some, m_ref[...] * scale + jnp.log(safe) * (1.0 / math.log(2.0)), NEG)
        pieces = []
        for row in to_lanes(level, rows):
            high = row.astype(BF16).astype(F32)
            mid = (row - high).astype(BF16).astype(F32)
            low = row - high - mid
            pieces += [high, mid, low]
        pad = jnp.zeros((META - len(pieces), 128), F32)
        o_ref[h, rows:, :] = jnp.concatenate(pieces + [pad], axis=0).astype(BF16)


def attend(q, keys, values, member, widths, scale, halves):
    homes, held, width = q.shape
    rows = held - META
    vmem = pl.BlockSpec(memory_space=pltpu.VMEM)
    smem = pl.BlockSpec(memory_space=pltpu.SMEM)
    return pl.pallas_call(
        functools.partial(attend_kernel, scale, halves),
        out_shape=jax.ShapeDtypeStruct(q.shape, BF16),
        in_specs=[smem, smem, vmem, vmem, vmem],
        out_specs=vmem,
        scratch_shapes=[pltpu.VMEM((rows, 1), F32), pltpu.VMEM((rows, 2 * width), F32)],
        compiler_params=pltpu.CompilerParams(vmem_limit_bytes=24 << 20),
        cost_estimate=pl.CostEstimate(flops=4 << 30, bytes_accessed=4 << 20, transcendentals=6 << 20),
        name="attend",
    )(member, widths, q, keys, values)


def own_kernel(scale, group, first, q_ref, k_ref, v_ref, o_ref):
    halves, part, width = q_ref.shape
    new = k_ref.shape[1]
    rows = halves * part
    for i in range(halves):
        s = lax.dot_general(q_ref[i], k_ref[i], (((1,), (1,)), ((), ())), preferred_element_type=F32)
        row = lax.broadcasted_iota(jnp.int32, (part, new), 0) // group
        position = first(row)
        seen = position >= lax.broadcasted_iota(jnp.int32, (part, new), 1)
        s = jnp.where(seen, s, NEG)
        peak = jnp.max(s, axis=1, keepdims=True)
        weights = jnp.where(seen, jnp.exp2((s - peak) * scale), 0.0)
        total = jnp.sum(weights, axis=1, keepdims=True)
        summed = jnp.dot(weights.astype(BF16), v_ref[i], preferred_element_type=F32)
        o_ref[i * part : (i + 1) * part, :] = summed / total
        level = peak * scale + jnp.log(total) * (1.0 / math.log(2.0))
        rowed = to_lanes(level, part)
        for b, line in enumerate(rowed):
            at = rows + i * len(rowed) + b
            o_ref[at : at + 1, :] = line


def own_part(q, keys, values, scale, group, first):
    halves, part, width = q.shape
    vmem = pl.BlockSpec(memory_space=pltpu.VMEM)
    return pl.pallas_call(
        functools.partial(own_kernel, scale, group, first),
        out_shape=jax.ShapeDtypeStruct((halves * part + 8, width), F32),
        in_specs=[vmem] * 3,
        out_specs=vmem,
        cost_estimate=pl.CostEstimate(flops=1 << 22, bytes_accessed=1 << 18, transcendentals=1 << 14),
        name="own",
    )(q, keys, values)


def project_kernel(group, a_ref, own_ref, w_ref, o_ref, sum_ref, flat_ref):
    owners = a_ref.shape[0]
    rows = a_ref.shape[1] - META
    width = a_ref.shape[2]

    @pl.when(pl.program_id(0) == 0)
    def _():
        for b in range(rows // 128):
            lines = [own_ref[rows + b : rows + b + 1, :]]
            for o in range(owners):
                meta = a_ref[o, rows:, :].astype(F32)
                lines.append(meta[3 * b : 3 * b + 1] + meta[3 * b + 1 : 3 * b + 2] + meta[3 * b + 2 : 3 * b + 3])
            level = jnp.concatenate(lines + [jnp.full((128 - len(lines), 128), NEG, F32)], axis=0)
            top = jnp.max(level, axis=0, keepdims=True)
            weight = jnp.exp2(level - top)
            weight = weight / jnp.sum(weight, axis=0, keepdims=True)
            weight = weight.T
            here = slice(b * 128, (b + 1) * 128)
            acc = own_ref[here, :] * weight[:, 0:1]
            for o in range(owners):
                acc = acc + a_ref[o, here, :].astype(F32) * weight[:, o + 1 : o + 2]
            sum_ref[here, :] = acc
        for g in range(group):
            flat_ref[:, g * width : (g + 1) * width] = sum_ref[pl.ds(g, rows // group, stride=group), :].astype(BF16)

    o_ref[...] = jnp.dot(flat_ref[...], w_ref[...], preferred_element_type=F32).astype(BF16)


def project(arrived, own, weight, group):
    owners, held, width = arrived.shape
    rows = held - META
    depth, columns = weight.shape
    block = 1024
    return pl.pallas_call(
        functools.partial(project_kernel, group),
        out_shape=jax.ShapeDtypeStruct((rows // group, columns), BF16),
        grid=(columns // block,),
        in_specs=[
            pl.BlockSpec(arrived.shape, lambda j: (0, 0, 0)),
            pl.BlockSpec(own.shape, lambda j: (0, 0)),
            pl.BlockSpec((depth, block), lambda j: (0, j)),
        ],
        out_specs=pl.BlockSpec((rows // group, block), lambda j: (0, j)),
        scratch_shapes=[pltpu.VMEM((rows, width), F32), pltpu.VMEM((rows // group, depth), BF16)],
        compiler_params=pltpu.CompilerParams(vmem_limit_bytes=24 << 20),
        cost_estimate=pl.CostEstimate(flops=1 << 29, bytes_accessed=18 << 20, transcendentals=1 << 15),
        name="project",
    )(arrived, own, weight)


def local(
    queries, new_keys, new_values, ancestors, tile_keys, tile_values, tile_lengths, out_weight
):
    owners = lax.axis_size("owner")
    ranks = lax.axis_size("kvh")
    parts, new, group, width = queries.shape
    per_owner, size = tile_keys.shape[0], tile_keys.shape[2]
    tiles = per_owner * owners
    scale = width**-0.5 / math.log(2.0)
    share = parts * new // ranks
    piece = share // CHUNKS
    stretch = new // share
    split = queries.reshape(parts, stretch, CHUNKS, piece * group, width)

    member = jnp.any(ancestors[:, :, None] == jnp.arange(tiles, dtype=jnp.int32)[None, None, :], axis=1)
    meta = jnp.pad(member.astype(BF16), ((0, META - parts), (0, width - tiles)))

    arrived = []
    for c in range(CHUNKS):
        rows = split[:, :, c].reshape(-1, width)
        both = jnp.concatenate([rows, meta], axis=0)
        copies = jnp.broadcast_to(both, (owners, *both.shape))
        arrived.append(lax.all_to_all(copies, "owner", split_axis=0, concat_axis=0, tiled=True))

    slots = jnp.arange(size, dtype=jnp.int32)
    live = (slots[None, :] < tile_lengths[:, None])[:, :, None]
    keys = jnp.where(live, tile_keys[:, 0], tile_keys[:, 0, :1])
    values = jnp.concatenate(
        [jnp.where(live, tile_values[:, 0], jnp.zeros((), BF16)), jnp.broadcast_to(live, (per_owner, size, width)).astype(BF16)],
        axis=2,
    )
    widths = (tile_lengths + (STEP - 1)) // STEP

    held = arrived[0].shape[1] - META
    flags = arrived[0][:, held : held + parts, :tiles]
    mine = lax.axis_index("owner") * per_owner
    flags = lax.dynamic_slice_in_dim(flags, mine, per_owner, 2).astype(jnp.int32).reshape(-1)

    owns, backs = [], []
    for c in range(CHUNKS):
        q = split[:, :, c].reshape(parts, stretch * piece * group, width)

        def place(token, c=c):
            return (token // piece) * share + c * piece + token % piece

        owns.append(own_part(q, new_keys[:, :, 0], new_values[:, :, 0], scale, group, place))
    for c in range(CHUNKS):
        out = attend(arrived[c], keys, values, flags, widths, scale, parts)
        backs.append(lax.all_to_all(out, "owner", split_axis=0, concat_axis=0, tiled=True))
    sums = []
    for c in range(CHUNKS):
        mixed = project(backs[c], owns[c], out_weight, group)
        mixed = mixed.reshape(ranks, piece, -1)
        got = lax.all_to_all(mixed, "kvh", split_axis=0, concat_axis=0, tiled=True)
        sums.append(got.astype(F32).sum(axis=0).astype(BF16))
    return jnp.concatenate(sums, axis=0)


def solution(mesh):
    return jax.shard_map(
        local,
        mesh=mesh,
        in_specs=(
            P("owner", None, "kvh", None),
            P("owner", None, "kvh", None),
            P("owner", None, "kvh", None),
            P("owner", None),
            P("owner", "kvh", None, None),
            P("owner", "kvh", None, None),
            P("owner"),
            P("kvh", None),
        ),
        out_specs=P(("owner", "kvh"), None),
        check_vma=False,
    )
```

time: 232 us -> 193 us (0.83)
  Pallas kernels: 0 us -> 71.9 us
  matrix products: 66.4 us -> 0 us
  other arithmetic: 54.9 us -> 2.99 us
  starting transfers between devices: 19.1 us -> 68.9 us
  blocking collectives: 25 us -> 0 us
  waiting for transfers between devices: 46.7 us -> 25.2 us
  local copies, waits for them, and re-layouts: 18.7 us -> 21.6 us
    pallas_call x0 -> x6, Pallas kernels: none -> 71.9 us  [the longest x2 56 us: attend(): pl.pallas_call(functools.partial(attend_kernel, scale, halves), out_shape...]
    dot_general x5 -> x0, matrix products: 66.4 us -> none  [the longest x1 35 us: owner_partial(): jnp.dot(flat, keys.reshape(count * size, width).T, preferred_element_type...]
    all_to_all x3 -> x6, starting transfers between devices: 19.1 us -> 68.9 us  [the longest x2 42.8 us: local(): lax.all_to_all(out, 'owner', split_axis=0, concat_axis=0, tiled=True)]
    convert_element_type x2 -> x1, other arithmetic: 49.4 us -> 0.07 us  [local(): jnp.broadcast_to(live, (per_owner, size, width)).astype(BF16)]
    all_to_all x1 -> x0, blocking collectives: 25 us -> none  [sent_and_summed(): lax.all_to_all(parts, axis, split_axis=0, concat_axis=0, tiled=True)]
    all_to_all x3 -> x6, waiting for transfers between devices: 46.7 us -> 25.2 us  [the longest x2 15.9 us: local(): lax.all_to_all(copies, 'owner', split_axis=0, concat_axis=0, tiled=True)]
    unnamed x14 -> x25, local copies, waits for them, and re-layouts: 1.2 us -> 15.8 us
    another operation x1 -> x0, local copies, waits for them, and re-layouts: 2.88 us -> none  [owner_partial(): flat = qrows.reshape(count_p * rows, width)]
  transfers between devices with their start and end apart: 3 -> 6, of which waited for: 2 -> 2; matrix products, arithmetic and copies ran while one was open for 12% -> 2% of each run, Pallas kernels for 0% -> 38%
where the time goes in v1:
time: 193 us; the launch traced here: 191 us
  Pallas kernels  71.9 us (37%)
  starting transfers between devices  68.9 us (36%)
  waiting for transfers between devices  25.2 us (13%)
  local copies, waits for them, and re-layouts  21.6 us (11%)
  other arithmetic  2.99 us (2%)
    pallas_call x2, Pallas kernels, attend(): pl.pallas_call(functools.partial(attend_kernel, scale, halves), out_shape...  56 us
    all_to_all x2, starting transfers between devices, local(): lax.all_to_all(out, 'owner', split_axis=0, concat_axis=0, tiled=True)  42.8 us
    all_to_all x2, waiting for transfers between devices, local(): lax.all_to_all(copies, 'owner', split_axis=0, concat_axis=0, tiled=True)  15.9 us
    unnamed x25, local copies, waits for them, and re-layouts  15.8 us
    all_to_all x2, starting transfers between devices, local(): got = lax.all_to_all(mixed, 'kvh', split_axis=0, concat_axis=0, tiled=True)  13.1 us
    all_to_all x2, starting transfers between devices, local(): lax.all_to_all(copies, 'owner', split_axis=0, concat_axis=0, tiled=True)  13 us
    pallas_call x2, Pallas kernels, project(): pl.pallas_call(functools.partial(project_kernel, group), out_shape=jax.Sh...  11.8 us
    all_to_all x2, waiting for transfers between devices, local(): got = lax.all_to_all(mixed, 'kvh', split_axis=0, concat_axis=0, tiled=True)  9.23 us
  transfers between devices with their start and end apart: 6, of which 2 were waited for; matrix products, arithmetic and copies ran while one was open for 2% of the time, Pallas kernels for 38%

profile of v1, /device:TPU:1, one launch (start us, length us, event | category | flops | bytes accessed | tf_op | source)
XLA Modules:
  0.0 190.8 jit_solution(12875322913237526070)
XLA Ops:
  1.8 1.2 broadcast_in_dim.44
  2.9 8.6 %all-to-all-start = ((bf16[16,272,128]{2,1,0:T(8,128)(2,1)}), bf16[16,272,128]{2,1,0:T(8,128)(2,1)S(1)}, u32[]{:S(2)}, u32[]{:S(2)}) async-start(bf16[16,272,128]{2,1,0:T(8,128)(2,1)} %broadcast_in_dim.44), calls=%async_computation | async-start | bytes 2228224 | tf_op jit(solution)/shard_map/all_to_all | solution.py:208
  11.7 15.9 %all-to-all-done.q_ref = bf16[16,272,128]{2,1,0:T(8,128)(2,1)S(1)} async-done(((bf16[16,272,128]{2,1,0:T(8,128)(2,1)}), bf16[16,272,128]{2,1,0:T(8,128)(2,1)S(1)}, u32[]{:S(2)}, u32[]{:S(2)}) %all-to-all-start) | async-done | bytes 1114144 | tf_op jit(solution)/shard_map/all_to_all | solution.py:208
  27.6 1.1 broadcast_in_dim.50
  28.8 4.4 %all-to-all-start.3 = ((bf16[16,272,128]{2,1,0:T(8,128)(2,1)}), bf16[16,272,128]{2,1,0:T(8,128)(2,1)}, u32[]{:S(2)}, u32[]{:S(2)}) async-start(bf16[16,272,128]{2,1,0:T(8,128)(2,1)} %broadcast_in_dim.50), calls=%async_computation.3 | async-start | bytes 2228224 | tf_op jit(solution)/shard_map/all_to_all | solution.py:208
  34.7 27.1 %attend.2 = bf16[16,272,128]{2,1,0:T(8,128)(2,1)S(1)} custom-call(s32[192]{0:T(256)S(1)} %reshape.43.member, s32[6]{0:T(128)S(1)} %and_select_fusion.widths, bf16[16,272,128]{2,1,0:T(8,128)(2,1)S(1)} %all-to-all-done.q_ref, bf16[6,512,128]{2,1,0:T(8,128)(2,1)S(1)} %get-tuple-element.8.k_ref, bf16[6,512,256]{2,1,0:T(8,128)(2,1)S(1)} %pad_maximum_fusion.v_ref), custom_call_target="tpu_custom_call" | custom-call | flops 4294967296 | bytes 4194304 | tf_op jit(solution)/shard_map/attend/pallas_call | solution.py:89
  61.8 1.0 copy-done.4
  62.8 20.9 %all-to-all-start.1 = ((bf16[16,272,128]{2,1,0:T(8,128)(2,1)}), bf16[16,272,128]{2,1,0:T(8,128)(2,1)S(1)}, u32[]{:S(2)}, u32[]{:S(2)}) async-start(bf16[16,272,128]{2,1,0:T(8,128)(2,1)} %copy-done.4), calls=%async_computation.1 | async-start | bytes 2228224 | tf_op jit(solution)/shard_map/all_to_all | solution.py:234
  83.7 1.4 copy-done.3
  85.1 28.9 %attend.3 = bf16[16,272,128]{2,1,0:T(8,128)(2,1)} custom-call(s32[192]{0:T(256)S(1)} %reshape.43.member, s32[6]{0:T(128)S(1)} %and_select_fusion.widths, bf16[16,272,128]{2,1,0:T(8,128)(2,1)} %all-to-all-done.3.q_ref, bf16[6,512,128]{2,1,0:T(8,128)(2,1)S(1)} %get-tuple-element.8.k_ref, bf16[6,512,256]{2,1,0:T(8,128)(2,1)S(1)} %copy-done.3), custom_call_target="tpu_custom_call" | custom-call | flops 4294967296 | bytes 4194304 | tf_op jit(solution)/shard_map/attend/pallas_call | solution.py:89
  114.0 21.9 %all-to-all-start.4 = ((bf16[16,272,128]{2,1,0:T(8,128)(2,1)}), bf16[16,272,128]{2,1,0:T(8,128)(2,1)S(1)}, u32[]{:S(2)}, u32[]{:S(2)}) async-start(bf16[16,272,128]{2,1,0:T(8,128)(2,1)} %attend.3), calls=%async_computation.4 | async-start | bytes 2228224 | tf_op jit(solution)/shard_map/all_to_all | solution.py:234
  135.9 2.1 %own.2.own_ref = f32[264,128]{1,0:T(8,128)} custom-call(bf16[2,128,128]{2,1,0:T(8,128)(2,1)} %bitcast.23, bf16[2,32,128]{2,1,0:T(8,128)(2,1)} %bitcast.25, bf16[2,32,128]{2,1,0:T(8,128)(2,1)} %bitcast.27), custom_call_target="tpu_custom_call" | custom-call | flops 4194304 | bytes 262144 | tf_op jit(solution)/shard_map/own/pallas_call | solution.py:126
  138.0 5.8 %copy-done = bf16[1024,8192]{1,0:T(8,128)(2,1)S(1)} copy-done((bf16[1024,8192]{1,0:T(8,128)(2,1)S(1)}, bf16[1024,8192]{1,0:T(8,128)(2,1)}, u32[]{:S(2)}) %copy-start) | copy-done | bytes 16777240
  143.8 0.9 copy-done.5
  144.7 5.9 %project.2 = bf16[32,8192]{1,0:T(8,128)(2,1)S(1)} custom-call(bf16[16,272,128]{2,1,0:T(8,128)(2,1)S(1)} %all-to-all-done.1.a_ref, f32[264,128]{1,0:T(8,128)S(1)} %copy-done.5, bf16[1024,8192]{1,0:T(8,128)(2,1)S(1)} %copy-done), custom_call_target="tpu_custom_call" | custom-call | flops 536870912 | bytes 18874368 | tf_op jit(solution)/shard_map/project/pallas_call | solution.py:169
  150.6 1.0 reshape.40
  151.6 8.3 %all-to-all-start.2 = ((bf16[8,4,8192]{2,1,0:T(4,128)(2,1)}), bf16[8,4,8192]{2,1,0:T(4,128)(2,1)S(1)}, u32[]{:S(2)}, u32[]{:S(2)}) async-start(bf16[8,4,8192]{2,1,0:T(4,128)(2,1)} %reshape.40), calls=%async_computation.2 | async-start | bytes 1048576 | tf_op jit(solution)/shard_map/all_to_all | solution.py:239
  159.8 2.1 %own.3.own_ref = f32[264,128]{1,0:T(8,128)} custom-call(bf16[2,128,128]{2,1,0:T(8,128)(2,1)} %bitcast.21, bf16[2,32,128]{2,1,0:T(8,128)(2,1)} %bitcast.26, bf16[2,32,128]{2,1,0:T(8,128)(2,1)} %bitcast.28), custom_call_target="tpu_custom_call" | custom-call | flops 4194304 | bytes 262144 | tf_op jit(solution)/shard_map/own/pallas_call | solution.py:126
  161.9 5.8 %copy-done.1 = bf16[1024,8192]{1,0:T(8,128)(2,1)S(1)} copy-done((bf16[1024,8192]{1,0:T(8,128)(2,1)S(1)}, bf16[1024,8192]{1,0:T(8,128)(2,1)}, u32[]{:S(2)}) %copy-start.1) | copy-done | bytes 16777240
  167.7 0.9 copy-done.6
  168.6 5.9 %project.3 = bf16[32,8192]{1,0:T(8,128)(2,1)S(1)} custom-call(bf16[16,272,128]{2,1,0:T(8,128)(2,1)S(1)} %all-to-all-done.4.a_ref, f32[264,128]{1,0:T(8,128)S(1)} %copy-done.6, bf16[1024,8192]{1,0:T(8,128)(2,1)S(1)} %copy-done.1), custom_call_target="tpu_custom_call" | custom-call | flops 536870912 | bytes 18874368 | tf_op jit(solution)/shard_map/project/pallas_call | solution.py:169
  174.5 1.0 reshape.41
  175.5 4.8 %all-to-all-start.5 = ((bf16[8,4,8192]{2,1,0:T(4,128)(2,1)}), bf16[8,4,8192]{2,1,0:T(4,128)(2,1)S(1)}, u32[]{:S(2)}, u32[]{:S(2)}) async-start(bf16[8,4,8192]{2,1,0:T(4,128)(2,1)} %reshape.41), calls=%async_computation.5 | async-start | bytes 1048576 | tf_op jit(solution)/shard_map/all_to_all | solution.py:239
  180.6 9.2 %all-to-all-done.5 = bf16[8,4,8192]{2,1,0:T(4,128)(2,1)S(1)} async-done(((bf16[8,4,8192]{2,1,0:T(4,128)(2,1)}), bf16[8,4,8192]{2,1,0:T(4,128)(2,1)S(1)}, u32[]{:S(2)}, u32[]{:S(2)}) %all-to-all-start.5) | async-done | bytes 524320 | tf_op jit(solution)/shard_map/all_to_all | solution.py:239
  (39 shorter events, 4.5 us)
Async XLA Ops:
  0.9 0.9 copy-start.10
  0.9 2.1 %copy-start.9 = (bf16[2,4,1,32,128]{4,3,2,1,0:T(8,128)(2,1)}, bf16[2,4,1,32,128]{4,3,2,1,0:T(8,128)(2,1)S(1)}, u32[]{:S(2)}) copy-start(bf16[2,4,1,32,128]{4,3,2,1,0:T(8,128)(2,1)S(1)} %get-tuple-element.5) | copy-start | bytes 196612
  1.8 9.8 %copy-start.7 = (bf16[6,1,512,128]{3,2,1,0:T(8,128)(2,1)S(1)}, bf16[6,1,512,128]{3,2,1,0:T(8,128)(2,1)}, u32[]{:S(2)}) copy-start(bf16[6,1,512,128]{3,2,1,0:T(8,128)(2,1)} %param.12) | copy-start | bytes 2359300
  1.8 9.8 %copy-start.11 = (s32[6]{0:T(128)S(1)}, s32[6]{0:T(128)}, u32[]{:S(2)}) copy-start(s32[6]{0:T(128)} %param.14) | copy-start | bytes 76
  2.9 24.7 %all-to-all-start = ((bf16[16,272,128]{2,1,0:T(8,128)(2,1)}), bf16[16,272,128]{2,1,0:T(8,128)(2,1)S(1)}, u32[]{:S(2)}, u32[]{:S(2)}) async-start(bf16[16,272,128]{2,1,0:T(8,128)(2,1)} %broadcast_in_dim.44), calls=%async_computation | async-start | bytes 2228224 | tf_op jit(solution)/shard_map/all_to_all | solution.py:208
  27.6 5.5 %copy-start.8 = (bf16[6,1,512,128]{3,2,1,0:T(8,128)(2,1)S(1)}, bf16[6,1,512,128]{3,2,1,0:T(8,128)(2,1)}, u32[]{:S(2)}) copy-start(bf16[6,1,512,128]{3,2,1,0:T(8,128)(2,1)} %param.13) | copy-start | bytes 2359300
  28.8 34.0 %all-to-all-start.3 = ((bf16[16,272,128]{2,1,0:T(8,128)(2,1)}), bf16[16,272,128]{2,1,0:T(8,128)(2,1)}, u32[]{:S(2)}, u32[]{:S(2)}) async-start(bf16[16,272,128]{2,1,0:T(8,128)(2,1)} %broadcast_in_dim.50), calls=%async_computation.3 | async-start | bytes 2228224 | tf_op jit(solution)/shard_map/all_to_all | solution.py:208
  34.4 27.4 %copy-start.2 = (bf16[6,512,256]{2,1,0:T(8,128)(2,1)}, bf16[6,512,256]{2,1,0:T(8,128)(2,1)S(1)}, u32[]{:S(2)}) copy-start(bf16[6,512,256]{2,1,0:T(8,128)(2,1)S(1)} %pad_maximum_fusion.v_ref) | copy-start | bytes 4718596
  61.8 1.0 copy-start.4
  62.8 51.2 %all-to-all-start.1 = ((bf16[16,272,128]{2,1,0:T(8,128)(2,1)}), bf16[16,272,128]{2,1,0:T(8,128)(2,1)S(1)}, u32[]{:S(2)}, u32[]{:S(2)}) async-start(bf16[16,272,128]{2,1,0:T(8,128)(2,1)} %copy-done.4), calls=%async_computation.1 | async-start | bytes 2228224 | tf_op jit(solution)/shard_map/all_to_all | solution.py:234
  83.7 1.4 copy-start.3
  114.0 37.6 %all-to-all-start.4 = ((bf16[16,272,128]{2,1,0:T(8,128)(2,1)}), bf16[16,272,128]{2,1,0:T(8,128)(2,1)S(1)}, u32[]{:S(2)}, u32[]{:S(2)}) async-start(bf16[16,272,128]{2,1,0:T(8,128)(2,1)} %attend.3), calls=%async_computation.4 | async-start | bytes 2228224 | tf_op jit(solution)/shard_map/all_to_all | solution.py:234
  138.0 5.8 %copy-start = (bf16[1024,8192]{1,0:T(8,128)(2,1)S(1)}, bf16[1024,8192]{1,0:T(8,128)(2,1)}, u32[]{:S(2)}) copy-start(bf16[1024,8192]{1,0:T(8,128)(2,1)} %w_ref.3) | copy-start | bytes 50331652
  143.8 0.9 copy-start.5
  151.6 23.9 %all-to-all-start.2 = ((bf16[8,4,8192]{2,1,0:T(4,128)(2,1)}), bf16[8,4,8192]{2,1,0:T(4,128)(2,1)S(1)}, u32[]{:S(2)}, u32[]{:S(2)}) async-start(bf16[8,4,8192]{2,1,0:T(4,128)(2,1)} %reshape.40), calls=%async_computation.2 | async-start | bytes 1048576 | tf_op jit(solution)/shard_map/all_to_all | solution.py:239
  161.9 5.8 %copy-start.1 = (bf16[1024,8192]{1,0:T(8,128)(2,1)S(1)}, bf16[1024,8192]{1,0:T(8,128)(2,1)}, u32[]{:S(2)}) copy-start(bf16[1024,8192]{1,0:T(8,128)(2,1)} %w_ref.3) | copy-start | bytes 50331652
  167.7 0.9 copy-start.6
  175.5 14.3 %all-to-all-start.5 = ((bf16[8,4,8192]{2,1,0:T(4,128)(2,1)}), bf16[8,4,8192]{2,1,0:T(4,128)(2,1)S(1)}, u32[]{:S(2)}, u32[]{:S(2)}) async-start(bf16[8,4,8192]{2,1,0:T(4,128)(2,1)} %reshape.41), calls=%async_computation.5 | async-start | bytes 1048576 | tf_op jit(solution)/shard_map/all_to_all | solution.py:239
